TPU v7x, 32 devices: a whole 2x2x4 slice. The times are simulated.
32 devices in a mesh: blen: 4 (over z), tm: 8 (over y, x, core).
Axes of the slice: x: 2, y: 2, z: 4, core: 2. Of those that a mesh axis runs over, the one named last changes fastest.
Arguments:
- model_grid: bfloat16 [256, 2, 512, 512], P(('blen', 'tm')), may hold values from -6 to 6
- vis_values: float32 [2, 16384], P(None, ('blen', 'tm')), may hold values from -6 to 6
- weights: float32 [16384], P(('blen', 'tm')), may hold values from 0.3 to 3
- flags: int32 [16384], P(('blen', 'tm')), may hold values 0 or 1
- uv_frac: float32 [2, 16384], P(None, ('blen', 'tm')), may hold values from 0 to 1
- cell_offset: int32 [2, 16384], P(None, ('blen', 'tm')), may hold values from 3 to 507
- tile_index: int32 [16384, 1], P(('blen', 'tm')), may hold values from 0 to 255; in each aligned block of 512 rows (0 to 511, 512 to 1023, ...) at most 4 rows name the same one
Outputs:
- gradient: float32 [8192, 8192], P(('blen', 'tm'))
- weighted_residual: float32 [2, 16384], P(None, ('blen', 'tm'))
Inputs may be any that keep to these rules, and one draw needn't show every extreme that they name: `tile_index`: in the rows of one device no tile is named by more than 4 rows, and some device has a tile named by exactly 4 rows.
All inputs are finite; a program needn't handle non-finite values. No bound on the sum of `flags` on one device may be relied on, other than what follows from the above.
Results may differ from a plain program's by a relative error of at most 0.0095.
Values sent between devices are 32-bit elements; how exact they have to be, the bound alone decides.
No kernel may reach another device: no remote copies, remote signals or barrier semaphores. Data moves between devices by JAX's collectives and lax.ppermute only.
A program may use at most 192 MiB of HBM per device.

v0:
```python
import math
import jax
import jax.numpy as jnp
from jax import lax
from jax.sharding import PartitionSpec as P

NPIX = 8192
KSUP = 8
NT = 16
MOST = 4
kernel_scale = 0.5
highest = lax.Precision.HIGHEST


def taps_full(offsets, fractions, tile_side):
    cell_ids = lax.broadcasted_iota(jnp.int32, offsets.shape + (tile_side,), offsets.ndim)
    shifted = cell_ids - offsets[..., None]
    distance = shifted.astype(jnp.float32) - fractions[..., None]
    inside = (shifted >= 1 - KSUP // 2) & (shifted <= KSUP // 2)
    values = jnp.exp(-kernel_scale * distance * distance)
    return jnp.where(inside, values, 0.0).astype(jnp.bfloat16)


def phase_table(row_count, col_count, period):
    row_ids = lax.broadcasted_iota(jnp.int32, (row_count, col_count), 0)
    col_ids = lax.broadcasted_iota(jnp.int32, (row_count, col_count), 1)
    angles = 2.0 * math.pi / period * (row_ids * col_ids % period).astype(jnp.float32)
    return (jnp.cos(angles), jnp.sin(angles))


def complex_block(cos_part, sin_part):
    return jnp.stack([jnp.stack([cos_part, -sin_part]), jnp.stack([sin_part, cos_part])])


def on_device(model_grid, vis_values, weights, flags, uv_frac, cell_offset, tile_index):
    blen_size = lax.axis_size("blen")
    tm_size = lax.axis_size("tm")
    devices = blen_size * tm_size
    per_dev = model_grid.shape[0]
    tile_side = model_grid.shape[2]
    vis_count = weights.shape[0]
    ntiles = per_dev * devices
    total_slots = ntiles * MOST
    tile_ids = tile_index[:, 0]
    matches = tile_ids[:, None] == lax.broadcasted_iota(jnp.int32, (vis_count, ntiles), 1)
    counts = jnp.sum(matches.astype(jnp.int32), axis=0)
    starts = jnp.cumsum(counts) - counts
    sorting = jnp.argsort(tile_ids, stable=True)
    position = (
        jnp.zeros((vis_count,), jnp.int32).at[sorting].set(jnp.arange(vis_count, dtype=jnp.int32))
    )
    first_slot = jnp.sum(jnp.where(matches, starts[None, :], 0), axis=1)
    rank_in_tile = position - first_slot
    owner_dev = tile_ids // per_dev
    local_tile = tile_ids % per_dev
    slot_of = (local_tile * devices + owner_dev) * MOST + rank_in_tile
    weighted = weights * flags.astype(jnp.float32)
    float_fields = jnp.stack([vis_values[0], vis_values[1], weighted, uv_frac[0], uv_frac[1]])
    send_float = jnp.zeros((5, total_slots), jnp.float32).at[:, slot_of].set(float_fields)
    send_int = jnp.zeros((2, total_slots), jnp.int32).at[:, slot_of].set(cell_offset)
    recv_float, recv_int = (
        lax.all_to_all(
            send_float.reshape(5, per_dev, devices, MOST),
            ("blen", "tm"),
            split_axis=2,
            concat_axis=2,
            tiled=True,
        ),
        lax.all_to_all(
            send_int.reshape(2, per_dev, devices, MOST),
            ("blen", "tm"),
            split_axis=2,
            concat_axis=2,
            tiled=True,
        ),
    )
    owner_rows = devices * MOST
    block_rows = 512 if owner_rows % 512 == 0 else owner_rows
    block_count = owner_rows // block_rows
    float_blocks = recv_float.reshape(5, per_dev, block_count, block_rows).transpose(2, 0, 1, 3)
    int_blocks = recv_int.reshape(2, per_dev, block_count, block_rows).transpose(2, 0, 1, 3)

    def grid_step(adjoint, inputs):
        part_float, part_int = inputs
        taps_u = taps_full(part_int[0], part_float[3], tile_side)
        taps_v = taps_full(part_int[1], part_float[4], tile_side)
        partial_sums = jnp.einsum(
            "qrj,qcji->qrci", taps_v, model_grid, preferred_element_type=jnp.float32
        )
        predicted = jnp.sum(partial_sums * taps_u[:, :, None, :], axis=-1)
        observed = jnp.stack([part_float[0], part_float[1]], axis=-1)
        residual = part_float[2][..., None] * (predicted - observed)
        spread = (residual[..., None] * taps_u[:, :, None, :]).astype(jnp.bfloat16)
        adjoint = adjoint + jnp.einsum(
            "qrj,qrci->qcji", taps_v, spread, preferred_element_type=jnp.float32
        )
        return (adjoint, jnp.moveaxis(residual, -1, 0))

    start_adjoint = jnp.zeros((per_dev, 2, tile_side, tile_side), jnp.float32)
    adjoint, residual_blocks = lax.scan(grid_step, start_adjoint, (float_blocks, int_blocks))
    residual_slots = residual_blocks.transpose(1, 2, 0, 3).reshape(2, per_dev, owner_rows)
    returned = lax.all_to_all(
        residual_slots.reshape(2, per_dev, devices, MOST),
        ("blen", "tm"),
        split_axis=2,
        concat_axis=2,
        tiled=True,
    )
    weighted_residual = returned.reshape(2, total_slots)[:, slot_of]
    relaid = lax.all_to_all(adjoint, "tm", split_axis=2, concat_axis=0, tiled=True)
    tile_cols = NT // blen_size
    col_slice = tile_side // tm_size
    pieces = relaid.reshape(NT, tile_cols, 2, col_slice, tile_side)
    cos_small, sin_small = phase_table(NT, NT, NT)
    small_turn = complex_block(cos_small, sin_small)
    cos_twist, sin_twist = phase_table(NT, tile_side, NPIX)
    cos_tile, sin_tile = phase_table(tile_side, tile_side, tile_side)
    tile_turn = complex_block(cos_tile, sin_tile)
    section_one = jnp.einsum("acnt,tvcji->anvji", small_turn, pieces, precision=highest)
    twist_c = cos_twist[:, None, None, :]
    twist_s = sin_twist[:, None, None, :]
    turned = jnp.stack(
        [
            section_one[0] * twist_c - section_one[1] * twist_s,
            section_one[0] * twist_s + section_one[1] * twist_c,
        ]
    )
    columns = jnp.einsum("acmi,cnvji->amnvj", tile_turn, turned, precision=highest)
    rows_dev = NPIX // devices
    spread_cols = rows_dev * tile_cols * col_slice
    packed = columns.reshape(2, 1, devices, spread_cols)
    landed = lax.all_to_all(packed, ("blen", "tm"), split_axis=2, concat_axis=1, tiled=True)
    landed = landed.reshape(2, blen_size, tm_size, rows_dev, tile_cols, col_slice)
    small_split = small_turn.reshape(2, 2, NT, blen_size, tile_cols)
    section_two = jnp.einsum("acnpv,cptrvj->antrj", small_split, landed, precision=highest)
    twist_cv = cos_twist.reshape(NT, tm_size, 1, col_slice)
    twist_sv = sin_twist.reshape(NT, tm_size, 1, col_slice)
    turned_rows = jnp.stack(
        [
            section_two[0] * twist_cv - section_two[1] * twist_sv,
            section_two[0] * twist_sv + section_two[1] * twist_cv,
        ]
    )
    real_turn = jnp.stack([cos_tile, -sin_tile]).reshape(2, tile_side, tm_size, col_slice)
    image_rows = jnp.einsum("cmtj,cntrj->rmn", real_turn, turned_rows, precision=highest)
    gradient = image_rows.reshape(rows_dev, NPIX) / NPIX
    return (gradient, weighted_residual)


def solution(mesh):
    in_specs = (
        P(("blen", "tm"), None, None, None),
        P(None, ("blen", "tm")),
        P(("blen", "tm")),
        P(("blen", "tm")),
        P(None, ("blen", "tm")),
        P(None, ("blen", "tm")),
        P(("blen", "tm"), None),
    )
    out_specs = (P(("blen", "tm"), None), P(None, ("blen", "tm")))
    return jax.shard_map(
        on_device, mesh=mesh, in_specs=in_specs, out_specs=out_specs, check_vma=False
    )
```

profile of v0, /device:TPU:0, one launch (start us, length us, event | category | flops | bytes accessed | tf_op | source)
XLA Modules:
  0.0 1047.1 jit_solution(14593329809357333968)
XLA Ops:
  14.8 7.3 all-to-all-start.1
  33.3 7.1 all-to-all-done
  43.2 5.3 multiply_reduce_fusion
  48.5 7.2 convolution_bitcast_fusion
  55.7 25.1 %copy.78 = f32[8,2,512,512]{3,1,0,2:T(2,128)} copy(f32[8,2,512,512]{2,3,1,0:T(8,128)} %convolution_bitcast_fusion) | data formatting | bytes 33554432 | tf_op jit(solution)/shard_map/while/body/eval_jaxpr/qrj,qrci->qcji/transpose | solution.py:94
  80.8 6.0 all-to-all-start.2
  97.8 173.0 %all-to-all-done.2 = f32[8,2,512,512]{3,1,0,2:T(2,128)} async-done(((f32[8,2,512,512]{3,1,0,2:T(2,128)}), f32[8,2,512,512]{3,1,0,2:T(2,128)}, u32[]{:S(2)}, u32[]{:S(2)}) %all-to-all-start.2) | async-done | bytes 16777248 | tf_op jit(solution)/shard_map/all_to_all | solution.py:110
  273.4 11.0 %copy.79 = f32[8,2,512,512]{3,2,1,0:T(8,128)S(1)} copy(f32[8,2,512,512]{3,1,0,2:T(2,128)} %all-to-all-done.2) | data formatting | bytes 33554432 | tf_op jit(solution)/shard_map/all_to_all | solution.py:110
  284.4 6.7 copy.80
  291.1 42.0 %fusion.11 = f32[2,16,4,64,512]{4,1,3,2,0:T(8,128)} fusion(f32[16,4,2,64,512]{4,3,2,1,0:T(8,128)} %bitcast.109, f32[1,2,16,16]{3,2,1,0:T(8,128)S(1)} %get-tuple-element.44, f32[1,2,16,16]{3,2,1,0:T(8,128)S(1)} %get-tuple-element.43), kind=kOutput, calls=%fused_computation.23 | convolution fusion | flops 1610613760 | bytes 33558528 | tf_op jit(solution)/shard_map/acnt,tvcji->anvji/dot_general | solution.py:119
  333.1 7.1 multiply_subtract_fusion.1
  340.2 6.4 pad_maximum_fusion
  346.6 67.2 %fusion.14 = f32[2,512,16,4,64]{1,4,3,2,0:T(8,128)} fusion(f32[2,16,4,64,512]{4,1,3,2,0:T(8,128)} %pad_maximum_fusion, f32[1,2,512,512]{3,2,1,0:T(8,128)S(1)} %copy-done, f32[1,2,512,512]{3,2,1,0:T(8,128)S(1)} %get-tuple-element.34), kind=kOutput, calls=%fused_computation.24 | convolution fusion | flops 51540656128 | bytes 37748736 | tf_op jit(solution)/shard_map/acmi,cnvji->amnvj/dot_general | solution.py:128
  413.8 31.1 %copy.83 = f32[2,512,16,4,64]{4,3,2,1,0:T(4,128)} copy(f32[2,512,16,4,64]{1,4,3,2,0:T(8,128)} %fusion.14) | data formatting | bytes 33554432 | tf_op jit(solution)/shard_map/acmi,cnvji->amnvj/dot_general | solution.py:128
  444.9 27.4 %reshape.436 = f32[2,1,32,65536]{3,2,0,1:T(8,128)} reshape(f32[2,512,16,4,64]{4,3,2,1,0:T(4,128)} %copy.83) | data formatting | bytes 33554432 | tf_op jit(solution)/shard_map/reshape | solution.py:131
  472.2 28.6 %copy.84 = f32[2,1,32,65536]{3,0,1,2:T(2,128)} copy(f32[2,1,32,65536]{3,2,0,1:T(8,128)} %reshape.436) | data formatting | bytes 33554432 | tf_op jit(solution)/shard_map/reshape | solution.py:131
  500.9 6.0 all-to-all-start.3
  516.5 363.0 %all-to-all-done.3 = f32[2,1,32,65536]{3,0,1,2:T(2,128)} async-done(((f32[2,1,32,65536]{3,0,1,2:T(2,128)}), f32[2,1,32,65536]{3,0,1,2:T(2,128)}, u32[]{:S(2)}, u32[]{:S(2)}) %all-to-all-start.3) | async-done | bytes 16777248 | tf_op jit(solution)/shard_map/all_to_all | solution.py:132
  879.5 38.4 %reshape.487 = f32[2,4,8,256,4,64]{5,4,3,0,2,1:T(4,128)} reshape(f32[2,1,32,65536]{3,0,1,2:T(2,128)} %all-to-all-done.3) | data formatting | bytes 33554432 | tf_op jit(solution)/shard_map/reshape | solution.py:133
  918.0 30.9 %copy.86 = f32[2,4,8,256,4,64]{3,4,1,0,5,2:T(4,128)} copy(f32[2,4,8,256,4,64]{5,4,3,0,2,1:T(4,128)} %reshape.487) | data formatting | bytes 33554432 | tf_op jit(solution)/shard_map/reshape | solution.py:133
  948.8 31.8 %fusion.17 = f32[2,16,8,256,64]{3,1,4,2,0:T(8,128)S(1)} fusion(f32[2,4,8,256,4,64]{3,4,1,0,5,2:T(4,128)} %copy.86, f32[2,2,16,4,4,1,1]{2,4,3,1,6,5,0:T(4,128)S(1)} %maximum_bitcast_fusion.17), kind=kOutput, calls=%fused_computation.25 | convolution fusion | flops 1610612736 | bytes 33558528 | tf_op jit(solution)/shard_map/acnpv,cptrvj->antrj/dot_general | solution.py:135
  985.2 42.3 %fusion.10 = f32[256,512,16]{1,0,2:T(8,128)} fusion(f32[2,16,8,256,64]{3,1,4,2,0:T(8,128)S(1)} %pad_maximum_fusion.1, f32[1,512,8,64]{1,3,2,0:T(8,128)S(1)} %get-tuple-element.56, f32[1,512,8,64]{1,3,2,0:T(8,128)S(1)} %get-tuple-element.57), kind=kOutput, calls=%fused_computation.18 | convolution fusion | flops 25772425216 | bytes 27262976 | tf_op jit(solution)/shard_map/cmtj,cntrj->rmn/dot_general | solution.py:145
  1027.6 10.3 copy.88
  1037.9 8.9 copy.92
  (68 shorter events, 55.8 us)
Async XLA Ops:
  11.4 14.1 %copy-start.1 = (s32[512]{0:T(512)}, s32[512]{0:T(512)S(1)}, u32[]{:S(2)}) copy-start(s32[512]{0:T(512)S(1)} %compare_select_fusion) | copy-start | bytes 6148
  14.8 15.5 %all-to-all-start.1 = ((s32[2,8,32,4]{1,3,0,2:T(4,128)}), s32[2,8,32,4]{1,3,0,2:T(4,128)S(1)}, u32[]{:S(2)}, u32[]{:S(2)}) async-start(s32[2,8,32,4]{1,3,0,2:T(4,128)} %copy.70), calls=%async_computation.1 | async-start | bytes 262144 | tf_op jit(solution)/shard_map/all_to_all | solution.py:69
  30.3 10.1 all-to-all-start
  80.8 190.0 %all-to-all-start.2 = ((f32[8,2,512,512]{3,1,0,2:T(2,128)}), f32[8,2,512,512]{3,1,0,2:T(2,128)}, u32[]{:S(2)}, u32[]{:S(2)}) async-start(f32[8,2,512,512]{3,1,0,2:T(2,128)} %copy.78), calls=%async_computation.2 | async-start | bytes 33554432 | tf_op jit(solution)/shard_map/all_to_all | solution.py:110
  270.8 230.0 %all-to-all-start.4 = ((f32[2,8,32,4]{1,3,0,2:T(4,128)}), f32[2,8,32,4]{1,3,0,2:T(4,128)S(1)}, u32[]{:S(2)}, u32[]{:S(2)}) async-start(f32[2,8,32,4]{1,3,0,2:T(4,128)} %copy.90), calls=%async_computation.4 | async-start | bytes 262144 | tf_op jit(solution)/shard_map/all_to_all | solution.py:102
  340.2 6.4 copy-start
  500.9 6.0 copy-start.2
  500.9 378.7 %all-to-all-start.3 = ((f32[2,1,32,65536]{3,0,1,2:T(2,128)}), f32[2,1,32,65536]{3,0,1,2:T(2,128)}, u32[]{:S(2)}, u32[]{:S(2)}) async-start(f32[2,1,32,65536]{3,0,1,2:T(2,128)} %copy.84), calls=%async_computation.3 | async-start | bytes 33554432 | tf_op jit(solution)/shard_map/all_to_all | solution.py:132
where the time goes:
time: 1060 us; the launch traced here: 1050 us
  waiting for transfers between devices  546 us (52%)
  local copies, waits for them, and re-layouts  235 us (22%)
  matrix products  196 us (18%)
  other arithmetic  44 us (4%)
  starting transfers between devices  24.7 us (2%)
    all_to_all x1, waiting for transfers between devices, on_device(): lax.all_to_all(packed, ('blen', 'tm'), split_axis=2, concat_axis=1, tiled...  363 us
    all_to_all x1, waiting for transfers between devices, on_device(): lax.all_to_all(adjoint, 'tm', split_axis=2, concat_axis=0, tiled=True)  173 us
    reshape x2, local copies, waits for them, and re-layouts, on_device(): landed.reshape(2, blen_size, tm_size, rows_dev, tile_cols, col_slice)  69.3 us
    dot_general x1, matrix products, on_device(): jnp.einsum('acmi,cnvji->amnvj', tile_turn, turned, precision=highest)  67.2 us
    reshape x2, local copies, waits for them, and re-layouts, on_device(): packed = columns.reshape(2, 1, devices, spread_cols)  56 us
    dot_general x1, matrix products, on_device(): jnp.einsum('cmtj,cntrj->rmn', real_turn, turned_rows, precision=highest)  42.3 us
    dot_general x1, matrix products, on_device(): jnp.einsum('acnt,tvcji->anvji', small_turn, pieces, precision=highest)  42 us
    dot_general x1, matrix products, on_device(): jnp.einsum('acnpv,cptrvj->antrj', small_split, landed, precision=highest)  31.8 us
  transfers between devices with their start and end apart: 5, of which 4 were waited for; matrix products, arithmetic and copies ran while one was open for 24% of the time, Pallas kernels for 0%

commit v1 on v0

--- a/solution.py
+++ b/solution.py
@@ -10,6 +10,17 @@
 MOST = 4
 kernel_scale = 0.5
 highest = lax.Precision.HIGHEST
+
+
+def cut_along(array, dim, peers):
+    before, after = (array.shape[:dim], array.shape[dim + 1 :])
+    return jnp.moveaxis(array.reshape(*before, peers, -1, *after), dim, 0)
+
+
+def joined_along(tiles, dim):
+    tiles = jnp.moveaxis(tiles, 0, dim)
+    shape = tiles.shape
+    return tiles.reshape(*shape[:dim], shape[dim] * shape[dim + 1], *shape[dim + 2 :])
 
 
 def taps_full(offsets, fractions, tile_side):
@@ -107,7 +118,15 @@
         tiled=True,
     )
     weighted_residual = returned.reshape(2, total_slots)[:, slot_of]
-    relaid = lax.all_to_all(adjoint, "tm", split_axis=2, concat_axis=0, tiled=True)
+    size, here = (lax.axis_size("tm"), lax.axis_index("tm"))
+    blocks = cut_along(adjoint, 2, size)
+    filled = blocks
+    for step in range(1, size):
+        target, source = ((here + step) % size, (here - step) % size)
+        sent = lax.dynamic_index_in_dim(blocks, target, 0)
+        partner_block = lax.ppermute(sent, "tm", [(i, (i + step) % size) for i in range(size)])
+        filled = lax.dynamic_update_slice_in_dim(filled, partner_block, source, axis=0)
+    relaid = joined_along(filled, 0)
     tile_cols = NT // blen_size
     col_slice = tile_side // tm_size
     pieces = relaid.reshape(NT, tile_cols, 2, col_slice, tile_side)

time: 1060 us -> 1020 us (0.962)
  waiting for transfers between devices: 546 us -> 470 us
  starting transfers between devices: 24.7 us -> 65.4 us
    all_to_all x1 -> x0, waiting for transfers between devices: 173 us -> none  [on_device(): lax.all_to_all(adjoint, 'tm', split_axis=2, concat_axis=0, tiled=True)]
    ppermute x0 -> x7, waiting for transfers between devices: none -> 97.5 us  [on_device(): lax.ppermute(sent, 'tm', [(i, (i + step) % size) for i in range(size)])]
    ppermute x0 -> x7, starting transfers between devices: none -> 46.6 us  [on_device(): lax.ppermute(sent, 'tm', [(i, (i + step) % size) for i in range(size)])]
    transpose x1 -> x0, local copies, waits for them, and re-layouts: 25.1 us -> none  [grid_step(): jnp.einsum('qrj,qrci->qcji', taps_v, spread, preferred_element_type=jnp.f...]
    dynamic_update_slice x0 -> x7, local copies, waits for them, and re-layouts: none -> 20.7 us  [on_device(): lax.dynamic_update_slice_in_dim(filled, partner_block, source, axis=0)]
    all_to_all x2 -> x0, local copies, waits for them, and re-layouts: 17.7 us -> none  [on_device(): lax.all_to_all(adjoint, 'tm', split_axis=2, concat_axis=0, tiled=True)]
    reshape x0 -> x1, local copies, waits for them, and re-layouts: none -> 12 us  [cut_along(): return jnp.moveaxis(array.reshape(*before, peers, -1, *after), dim, 0)]
    dynamic_slice x0 -> x1, local copies, waits for them, and re-layouts: none -> 11.1 us  [on_device(): sent = lax.dynamic_index_in_dim(blocks, target, 0)]
  transfers between devices with their start and end apart: 5 -> 11, of which waited for: 4 -> 7; matrix products, arithmetic and copies ran while one was open for 24% -> 26% of each run, Pallas kernels for 0% -> 0%
where the time goes in v1:
time: 1020 us; the launch traced here: 1010 us
  waiting for transfers between devices  470 us (46%)
  local copies, waits for them, and re-layouts  239 us (23%)
  matrix products  187 us (18%)
  starting transfers between devices  65.4 us (6%)
  other arithmetic  46.2 us (5%)
    all_to_all x1, waiting for transfers between devices, on_device(): lax.all_to_all(packed, ('blen', 'tm'), split_axis=2, concat_axis=1, tiled...  362 us
    ppermute x7, waiting for transfers between devices, on_device(): lax.ppermute(sent, 'tm', [(i, (i + step) % size) for i in range(size)])  97.5 us
    reshape x2, local copies, waits for them, and re-layouts, on_device(): landed.reshape(2, blen_size, tm_size, rows_dev, tile_cols, col_slice)  69.3 us
    dot_general x1, matrix products, on_device(): jnp.einsum('acmi,cnvji->amnvj', tile_turn, turned, precision=highest)  67 us
    reshape x2, local copies, waits for them, and re-layouts, on_device(): packed = columns.reshape(2, 1, devices, spread_cols)  55.8 us
    ppermute x7, starting transfers between devices, on_device(): lax.ppermute(sent, 'tm', [(i, (i + step) % size) for i in range(size)])  46.6 us
    dot_general x1, matrix products, on_device(): jnp.einsum('cmtj,cntrj->rmn', real_turn, turned_rows, precision=highest)  42.3 us
    dot_general x1, matrix products, on_device(): jnp.einsum('acnt,tvcji->anvji', small_turn, pieces, precision=highest)  33.1 us
  transfers between devices with their start and end apart: 11, of which 7 were waited for; matrix products, arithmetic and copies ran while one was open for 26% of the time, Pallas kernels for 0%

profile of v1, /device:TPU:0, one launch (start us, length us, event | category | flops | bytes accessed | tf_op | source)
XLA Modules:
  0.0 1008.7 jit_solution(15240779064843754211)
XLA Ops:
  14.8 7.3 all-to-all-start.1
  33.5 7.1 all-to-all-done
  52.0 7.1 fusion.30
  59.1 11.1 %dynamic-slice_bitcast_fusion = (f32[1,8,2,64,512]{4,3,2,1,0:T(8,128)S(1)}, f32[1,8,2,64,512]{4,3,2,1,0:T(8,128)}, f32[1,8,2,64,512]{4,3,2,1,0:T(8,128)}, f32[1,...) fusion(f32[8,2,8,64,512]{4,3,2,1,0:T(8,128)} %bitcast.127, ...), kind=kLoop, calls=%fused_computation.45 | loop fusion | bytes 29360156 | tf_op jit(solution)/shard_map/jit(dynamic_index_in_dim)/dynamic_slice | solution.py:126
  73.6 45.1 %collective-permute-done = f32[1,8,2,64,512]{4,3,2,1,0:T(8,128)S(1)} collective-permute-done((f32[1,8,2,64,512]{4,3,2,1,0:T(8,128)}, f32[1,8,2,64,512]{4,3,2,1,0:T(8,128)S(1)}, u32[]{:S(2)}, u32[]{:S(2)}) %collective-permute-start) | collective-permute-done | bytes 2097184 | tf_op jit(solution)/shard_map/ppermute | solution.py:127
  121.3 43.1 %collective-permute-start.6 = (f32[1,8,2,64,512]{4,3,2,1,0:T(8,128)S(1)}, f32[1,8,2,64,512]{4,3,2,1,0:T(8,128)}, u32[]{:S(2)}, u32[]{:S(2)}) collective-permute-start(f32[1,8,2,64,512]{4,3,2,1,0:T(8,128)S(1)} %get-tuple-element.34), channel_id=1, source_target_pairs={{0,7},{1,0},{2,1},{3,2},{4,3},{5,4},{6,5},{7,6},{8,15},{9,8},{10,9... | collective-permute-start | bytes 6291464 | tf_op jit(solution)/shard_map/ppermute | solution.py:127
  175.5 12.0 %copy.124 = f32[8,2,8,64,512]{4,3,1,0,2:T(8,128)} copy(f32[8,2,8,64,512]{4,3,2,1,0:T(8,128)} %bitcast.128) | data formatting | bytes 33554432 | tf_op jit(solution)/shard_map/reshape | solution.py:17
  195.9 14.3 %collective-permute-done.2 = f32[1,8,2,64,512]{4,3,2,1,0:T(8,128)} collective-permute-done((f32[1,8,2,64,512]{4,3,2,1,0:T(8,128)}, f32[1,8,2,64,512]{4,3,2,1,0:T(8,128)}, u32[]{:S(2)}, u32[]{:S(2)}) %collective-permute-start.2) | collective-permute-done | bytes 2097184 | tf_op jit(solution)/shard_map/ppermute | solution.py:127
  216.5 36.9 %collective-permute-done.4 = f32[1,8,2,64,512]{4,3,2,1,0:T(8,128)} collective-permute-done((f32[1,8,2,64,512]{4,3,2,1,0:T(8,128)}, f32[1,8,2,64,512]{4,3,2,1,0:T(8,128)}, u32[]{:S(2)}, u32[]{:S(2)}) %collective-permute-start.4) | collective-permute-done | bytes 2097184 | tf_op jit(solution)/shard_map/ppermute | solution.py:127
  262.9 33.1 %fusion.11 = f32[2,16,4,64,512]{4,1,3,2,0:T(8,128)} fusion(f32[16,4,2,64,512]{4,3,2,1,0:T(8,128)} %bitcast.130, f32[1,2,16,16]{3,2,1,0:T(8,128)S(1)} %get-tuple-element.51, f32[1,2,16,16]{3,2,1,0:T(8,128)S(1)} %get-tuple-element.50), kind=kOutput, calls=%fused_computation.23 | convolution fusion | flops 1610613760 | bytes 33558528 | tf_op jit(solution)/shard_map/acnt,tvcji->anvji/dot_general | solution.py:138
  296.0 7.1 multiply_subtract_fusion.1
  303.2 6.6 pad_maximum_fusion
  309.7 67.0 %fusion.14 = f32[2,512,16,4,64]{1,4,3,2,0:T(8,128)} fusion(f32[2,16,4,64,512]{4,1,3,2,0:T(8,128)} %pad_maximum_fusion, f32[1,2,512,512]{3,2,1,0:T(8,128)S(1)} %copy-done.1, f32[1,2,512,512]{3,2,1,0:T(8,128)S(1)} %copy-done), kind=kOutput, calls=%fused_computation.24 | convolution fusion | flops 51540656128 | bytes 37748736 | tf_op jit(solution)/shard_map/acmi,cnvji->amnvj/dot_general | solution.py:147
  376.7 31.1 %copy.82 = f32[2,512,16,4,64]{4,3,2,1,0:T(4,128)} copy(f32[2,512,16,4,64]{1,4,3,2,0:T(8,128)} %fusion.14) | data formatting | bytes 33554432 | tf_op jit(solution)/shard_map/acmi,cnvji->amnvj/dot_general | solution.py:147
  407.7 27.2 %reshape.442 = f32[2,1,32,65536]{3,2,0,1:T(8,128)} reshape(f32[2,512,16,4,64]{4,3,2,1,0:T(4,128)} %copy.82) | data formatting | bytes 33554432 | tf_op jit(solution)/shard_map/reshape | solution.py:150
  434.9 28.6 %copy.83 = f32[2,1,32,65536]{3,0,1,2:T(2,128)} copy(f32[2,1,32,65536]{3,2,0,1:T(8,128)} %reshape.442) | data formatting | bytes 33554432 | tf_op jit(solution)/shard_map/reshape | solution.py:150
  463.5 5.8 all-to-all-start.2
  479.0 362.1 %all-to-all-done.2 = f32[2,1,32,65536]{3,0,1,2:T(2,128)} async-done(((f32[2,1,32,65536]{3,0,1,2:T(2,128)}), f32[2,1,32,65536]{3,0,1,2:T(2,128)}, u32[]{:S(2)}, u32[]{:S(2)}) %all-to-all-start.2) | async-done | bytes 16777248 | tf_op jit(solution)/shard_map/all_to_all | solution.py:151
  841.1 38.4 %reshape.494 = f32[2,4,8,256,4,64]{5,4,3,0,2,1:T(4,128)} reshape(f32[2,1,32,65536]{3,0,1,2:T(2,128)} %all-to-all-done.2) | data formatting | bytes 33554432 | tf_op jit(solution)/shard_map/reshape | solution.py:152
  879.5 30.9 %copy.85 = f32[2,4,8,256,4,64]{3,4,1,0,5,2:T(4,128)} copy(f32[2,4,8,256,4,64]{5,4,3,0,2,1:T(4,128)} %reshape.494) | data formatting | bytes 33554432 | tf_op jit(solution)/shard_map/reshape | solution.py:152
  910.4 32.1 %fusion.17 = f32[2,16,8,256,64]{3,1,4,2,0:T(8,128)S(1)} fusion(f32[2,4,8,256,4,64]{3,4,1,0,5,2:T(4,128)} %copy.85, f32[2,2,16,4,4,1,1]{2,4,3,1,6,5,0:T(4,128)S(1)} %maximum_bitcast_fusion.17), kind=kOutput, calls=%fused_computation.25 | convolution fusion | flops 1610612736 | bytes 33558528 | tf_op jit(solution)/shard_map/acnpv,cptrvj->antrj/dot_general | solution.py:154
  947.1 42.3 %fusion.10 = f32[256,512,16]{1,0,2:T(8,128)} fusion(f32[2,16,8,256,64]{3,1,4,2,0:T(8,128)S(1)} %pad_maximum_fusion.1, f32[1,512,8,64]{1,3,2,0:T(8,128)S(1)} %get-tuple-element.63, f32[1,512,8,64]{1,3,2,0:T(8,128)S(1)} %get-tuple-element.64), kind=kOutput, calls=%fused_computation.18 | convolution fusion | flops 25772425216 | bytes 27262976 | tf_op jit(solution)/shard_map/cmtj,cntrj->rmn/dot_general | solution.py:164
  989.4 10.3 %copy.87 = f32[256,512,16]{0,2,1:T(8,128)} copy(f32[256,512,16]{1,0,2:T(8,128)} %fusion.10) | data formatting | bytes 16777216 | tf_op jit(solution)/shard_map/div | solution.py:165
  999.6 8.9 copy.91
  (91 shorter events, 92.0 us)
Async XLA Ops:
  14.8 15.5 %all-to-all-start.1 = ((s32[2,8,32,4]{1,3,0,2:T(4,128)}), s32[2,8,32,4]{1,3,0,2:T(4,128)S(1)}, u32[]{:S(2)}, u32[]{:S(2)}) async-start(s32[2,8,32,4]{1,3,0,2:T(4,128)} %copy.70), calls=%async_computation.1 | async-start | bytes 262144 | tf_op jit(solution)/shard_map/all_to_all | solution.py:80
  30.3 10.3 %all-to-all-start = ((f32[32,1,160]{2,1,0:T(1,128)}), f32[32,1,160]{2,1,0:T(1,128)S(1)}, u32[]{:S(2)}, u32[]{:S(2)}) async-start(f32[32,1,160]{2,1,0:T(1,128)} %reshape.502), calls=%async_computation | async-start | bytes 65536 | tf_op jit(solution)/shard_map/all_to_all | solution.py:73
  70.2 48.5 %collective-permute-start = (f32[1,8,2,64,512]{4,3,2,1,0:T(8,128)}, f32[1,8,2,64,512]{4,3,2,1,0:T(8,128)S(1)}, u32[]{:S(2)}, u32[]{:S(2)}) collective-permute-start(f32[1,8,2,64,512]{4,3,2,1,0:T(8,128)} %get-tuple-element.40), channel_id=1, source_target_pairs={{0,1},{1,2},{2,3},{3,4},{4,5},{5,6},{6,7},{7,0},{8,9},{9,10},{10,1... | collective-permute-start | bytes 6291464 | tf_op jit(solution)/shard_map/ppermute | solution.py:127
  70.3 49.7 %collective-permute-start.1 = (f32[1,8,2,64,512]{4,3,2,1,0:T(8,128)}, f32[1,8,2,64,512]{4,3,2,1,0:T(8,128)S(1)}, u32[]{:S(2)}, u32[]{:S(2)}) collective-permute-start(f32[1,8,2,64,512]{4,3,2,1,0:T(8,128)} %get-tuple-element.39), channel_id=1, source_target_pairs={{0,2},{1,3},{2,4},{3,5},{4,6},{5,7},{6,0},{7,1},{8,10},{9,11},{10,... | collective-permute-start | bytes 6291464 | tf_op jit(solution)/shard_map/ppermute | solution.py:127
  70.8 139.4 %collective-permute-start.2 = (f32[1,8,2,64,512]{4,3,2,1,0:T(8,128)}, f32[1,8,2,64,512]{4,3,2,1,0:T(8,128)}, u32[]{:S(2)}, u32[]{:S(2)}) collective-permute-start(f32[1,8,2,64,512]{4,3,2,1,0:T(8,128)} %get-tuple-element.38), channel_id=1, source_target_pairs={{0,3},{1,4},{2,5},{3,6},{4,7},{5,0},{6,1},{7,2},{8,11},{9,12},{10,... | collective-permute-start | bytes 6291464 | tf_op jit(solution)/shard_map/ppermute | solution.py:127
  72.3 141.0 %collective-permute-start.3 = (f32[1,8,2,64,512]{4,3,2,1,0:T(8,128)}, f32[1,8,2,64,512]{4,3,2,1,0:T(8,128)}, u32[]{:S(2)}, u32[]{:S(2)}) collective-permute-start(f32[1,8,2,64,512]{4,3,2,1,0:T(8,128)} %get-tuple-element.37), channel_id=1, source_target_pairs={{0,4},{1,5},{2,6},{3,7},{4,0},{5,1},{6,2},{7,3},{8,12},{9,13},{10,... | collective-permute-start | bytes 6291464 | tf_op jit(solution)/shard_map/ppermute | solution.py:127
  73.6 179.8 %collective-permute-start.4 = (f32[1,8,2,64,512]{4,3,2,1,0:T(8,128)}, f32[1,8,2,64,512]{4,3,2,1,0:T(8,128)}, u32[]{:S(2)}, u32[]{:S(2)}) collective-permute-start(f32[1,8,2,64,512]{4,3,2,1,0:T(8,128)} %get-tuple-element.36), channel_id=1, source_target_pairs={{0,5},{1,6},{2,7},{3,0},{4,1},{5,2},{6,3},{7,4},{8,13},{9,14},{10,... | collective-permute-start | bytes 6291464 | tf_op jit(solution)/shard_map/ppermute | solution.py:127
  118.7 1.3 copy-start.2
  118.7 137.9 %collective-permute-start.5 = (f32[1,8,2,64,512]{4,3,2,1,0:T(8,128)}, f32[1,8,2,64,512]{4,3,2,1,0:T(8,128)}, u32[]{:S(2)}, u32[]{:S(2)}) collective-permute-start(f32[1,8,2,64,512]{4,3,2,1,0:T(8,128)} %get-tuple-element.35), channel_id=1, source_target_pairs={{0,6},{1,7},{2,0},{3,1},{4,2},{5,3},{6,4},{7,5},{8,14},{9,15},{10,... | collective-permute-start | bytes 6291464 | tf_op jit(solution)/shard_map/ppermute | solution.py:127
  120.0 1.3 copy-start.3
  121.3 138.4 %collective-permute-start.6 = (f32[1,8,2,64,512]{4,3,2,1,0:T(8,128)S(1)}, f32[1,8,2,64,512]{4,3,2,1,0:T(8,128)}, u32[]{:S(2)}, u32[]{:S(2)}) collective-permute-start(f32[1,8,2,64,512]{4,3,2,1,0:T(8,128)S(1)} %get-tuple-element.34), channel_id=1, source_target_pairs={{0,7},{1,0},{2,1},{3,2},{4,3},{5,4},{6,5},{7,6},{8,15},{9,8},{10,9... | collective-permute-start | bytes 6291464 | tf_op jit(solution)/shard_map/ppermute | solution.py:127
  188.3 275.2 %all-to-all-start.3 = ((f32[2,8,32,4]{1,3,0,2:T(4,128)}), f32[2,8,32,4]{1,3,0,2:T(4,128)S(1)}, u32[]{:S(2)}, u32[]{:S(2)}) async-start(f32[2,8,32,4]{1,3,0,2:T(4,128)} %copy.89), calls=%async_computation.3 | async-start | bytes 262144 | tf_op jit(solution)/shard_map/all_to_all | solution.py:113
  191.0 3.3 copy-start.4
  303.1 6.6 copy-start
  303.1 6.6 copy-start.1
  463.5 377.5 %all-to-all-start.2 = ((f32[2,1,32,65536]{3,0,1,2:T(2,128)}), f32[2,1,32,65536]{3,0,1,2:T(2,128)}, u32[]{:S(2)}, u32[]{:S(2)}) async-start(f32[2,1,32,65536]{3,0,1,2:T(2,128)} %copy.83), calls=%async_computation.2 | async-start | bytes 33554432 | tf_op jit(solution)/shard_map/all_to_all | solution.py:151
